TPU v7x, 32 devices: a whole 2x2x4 slice. The times are simulated.
32 devices in a mesh: pole: 2 (over x), row: 8 (over z, y), col: 2 (over core).
Axes of the slice: x: 2, y: 2, z: 4, core: 2. Of those that a mesh axis runs over, the one named last changes fastest.
Arguments:
- ancestor_inverse: float32 [2, 24576, 12288], P(None, ('pole', 'row'), 'col'), parts along dimension 1, may hold values from -6 to 6
- factor_panels: float32 [4, 2, 24576, 128], P(None, None, ('pole', 'col', 'row')), parts along dimension 2, may hold values from -0.0546875 to 0.0546875
- diag_inverse: float32 [8, 2, 128, 128], P('pole'), parts along dimension 0, may hold values from -6 to 6
- coupling: float32 [4, 2, 128, 128], P('pole'), parts along dimension 0, may hold values from -0.5 to 0.5
- block_pattern: int32 [4, 96], replicated, may hold values from 0 to 1, as said below
- tree_order: int32 [4], replicated, may hold values from 0 to 3, each once
Outputs:
- inverse_panels: float32 [4, 2, 24576, 128], P(None, None, ('pole', 'row')), parts along dimension 2
- inverse_diagonal: float32 [8, 2, 128, 128], P('pole'), parts along dimension 0
- inverse_coupling: float32 [4, 2, 128, 128], P('pole'), parts along dimension 0
There are 2 independent parts, one for each index of `pole`. A program takes and returns all parts, laid end to end along the dimension named above; an argument that names none is the same for every part. Nothing has to cross between parts.
Inputs may be any that keep to these rules, and one draw needn't show every extreme that they name: `tree_order`: each supernode number appears once. `block_pattern`: blocks 0 and 48 lie in every supernode's structure.
All inputs are finite; a program needn't handle non-finite values.
Results may differ from a plain program's by a relative error of at most 0.0001.
Values sent between devices are 32-bit elements; how exact they have to be, the bound alone decides.
A program may use at most 192 MiB of HBM per device.

v0:
```python
import jax
import jax.numpy as jnp
from jax import lax
from jax.sharding import PartitionSpec as P


def swapped(block, axis, bit):
    count = lax.axis_size(axis)
    route = []
    for low in range(count):
        high = low | 1 << bit
        if high != low and high < count:
            route += [(low, high), (high, low)]
    return lax.ppermute(block, axis, route)


def matmul(left_side, right_side):
    return jnp.dot(
        left_side, right_side, preferred_element_type=jnp.float32, precision=lax.Precision.HIGHEST
    )


def multiply(left_side, right_side):
    real_part = matmul(left_side[0], right_side[0]) - matmul(left_side[1], right_side[1])
    imag_part = matmul(left_side[0], right_side[1]) + matmul(left_side[1], right_side[0])
    return jnp.stack([real_part, imag_part])


def flipped(matrix):
    return jnp.swapaxes(matrix, 1, 2)


def row_masks(pattern_eff, first_row, row_count, block_rows):
    row_index = first_row + jnp.arange(row_count, dtype=jnp.int32)
    blocks = row_index // block_rows
    onehot = (blocks[:, None] == jnp.arange(pattern_eff.shape[1], dtype=jnp.int32)[None, :]).astype(
        jnp.float32
    )
    return matmul(pattern_eff, onehot.T)


def per_device(ancestor_inverse, factor_panels, diag_inverse, coupling, block_pattern, tree_order):
    grid_row = lax.axis_index("row")
    grid_col = lax.axis_index("col")
    tile_rows = ancestor_inverse.shape[1]
    half_rows = ancestor_inverse.shape[2]
    piece_rows = factor_panels.shape[2]
    block_rows = factor_panels.shape[3]
    super_count = factor_panels.shape[0]
    share_rows = tile_rows // 2
    sorted_pattern = jnp.take(block_pattern, tree_order, axis=0).astype(jnp.float32)
    pattern_eff = jnp.concatenate(
        [sorted_pattern[:2], sorted_pattern[2:] * sorted_pattern[:2]], axis=0
    )
    source_mask = row_masks(
        pattern_eff, grid_col * half_rows + grid_row * piece_rows, piece_rows, block_rows
    )
    target_mask = row_masks(pattern_eff, grid_row * tile_rows, tile_rows, block_rows)
    panels = jnp.take(factor_panels, tree_order, axis=0) * source_mask[:, None, :, None]
    diag_blocks = jnp.take(diag_inverse, tree_order, axis=0)
    columns = []
    products = []
    for tree_slot in range(super_count):
        gathered = lax.all_gather(panels[tree_slot], "row", axis=1, tiled=True)
        columns.append(gathered)
        products.append(lax.psum(multiply(ancestor_inverse, gathered), "col"))
    own_flag = (grid_row * tile_rows // half_rows == grid_col).astype(jnp.float32)
    offset = jnp.clip(grid_row * tile_rows - grid_col * half_rows, 0, half_rows - tile_rows)
    own_windows = jnp.stack(
        [
            lax.dynamic_slice_in_dim(column_set, offset, tile_rows, 1) * own_flag
            for column_set in columns
        ]
    )
    partner_windows = swapped(own_windows, "col", 0)
    tile_windows = own_windows + partner_windows

    def share(matrix):
        return lax.dynamic_slice_in_dim(matrix, grid_col * share_rows, share_rows, 1)

    windows = [share(tile_windows[tree_slot]) for tree_slot in range(super_count)]
    parent_cols = [
        -target_mask[tree_slot][None, :, None] * products[tree_slot] for tree_slot in range(2)
    ]
    child_cols = [
        -target_mask[tree_slot + 2][None, :, None]
        * (products[tree_slot + 2] + multiply(parent_cols[tree_slot], coupling[tree_slot]))
        for tree_slot in range(2)
    ]
    parent_local = [
        multiply(flipped(windows[tree_slot]), share(parent_cols[tree_slot]))
        for tree_slot in range(2)
    ]
    cross_local = [
        multiply(flipped(share(parent_cols[tree_slot])), windows[tree_slot + 2])
        for tree_slot in range(2)
    ]
    child_local = [
        multiply(flipped(windows[tree_slot + 2]), share(child_cols[tree_slot]))
        for tree_slot in range(2)
    ]
    parent_sums = lax.psum(jnp.stack(parent_local), ("row", "col"))
    parent_diag = [diag_blocks[tree_slot] - parent_sums[tree_slot] for tree_slot in range(2)]
    child_totals = lax.psum(jnp.stack(cross_local + child_local), ("row", "col"))
    crosses = [
        -(child_totals[tree_slot] + multiply(parent_diag[tree_slot], coupling[tree_slot]))
        for tree_slot in range(2)
    ]
    child_sums = [child_totals[2 + tree_slot] for tree_slot in range(2)]
    child_diag = [
        diag_blocks[tree_slot + 2]
        - child_sums[tree_slot]
        - multiply(flipped(coupling[tree_slot]), crosses[tree_slot])
        for tree_slot in range(2)
    ]
    all_cols = jnp.stack(parent_cols + child_cols)
    all_diag = jnp.stack(parent_diag + child_diag)
    inverse_panels = jnp.zeros_like(all_cols).at[tree_order].set(all_cols)
    inverse_diagonal = jnp.zeros_like(all_diag).at[tree_order].set(all_diag)
    return (inverse_panels, inverse_diagonal, jnp.stack(crosses))


def solution(mesh):
    return jax.shard_map(
        per_device,
        mesh=mesh,
        in_specs=(
            P(None, ("pole", "row"), "col"),
            P(None, None, ("pole", "col", "row"), None),
            P("pole", None, None, None),
            P("pole", None, None, None),
            P(),
            P(),
        ),
        out_specs=(
            P(None, None, ("pole", "row"), None),
            P("pole", None, None, None),
            P("pole", None, None, None),
        ),
        check_vma=False,
    )
```

profile of v0, /device:TPU:0, one launch (start us, length us, event | category | flops | bytes accessed | tf_op | source)
XLA Modules:
  0.0 873.5 jit_solution(7536772676169645142)
XLA Ops:
  10.7 2.4 gather_fusion.1
  13.5 2.4 select_multiply_fusion
  19.7 99.5 %all-gather.11.cloned.1.call-done = f32[1,2,6144,128]{3,2,1,0:T(8,128)} async-done(((f32[1,2,768,128]{3,2,1,0:T(8,128)}), f32[1,2,6144,128]{3,2,1,0:T(8,128)}) %all-gather.11.cloned.1.call-update) | async-done | bytes 6291472 | tf_op jit(solution)/shard_map/all_gather | solution.py:64
  119.2 36.1 %fusion.8 = f32[128,1536]{1,0:T(8,128)S(1)} fusion(f32[2,1536,6144]{2,1,0:T(8,128)} %param.6, f32[1,2,6144,128]{3,2,1,0:T(8,128)} %all-gather.11.cloned.1.call-done), kind=kOutput, calls=%fused_computation.13 | convolution fusion | flops 14495514624 | bytes 41680896 | tf_op jit(solution)/shard_map/dot_general | solution.py:18
  155.3 35.0 %fusion.10 = f32[128,1536]{1,0:T(8,128)S(1)} fusion(f32[2,1536,6144]{2,1,0:T(8,128)} %param.6, f32[1,2,6144,128]{3,2,1,0:T(8,128)S(1)} %copy-done.2), kind=kOutput, calls=%fused_computation.15 | convolution fusion | flops 14495514624 | bytes 41680896 | tf_op jit(solution)/shard_map/dot_general | solution.py:18
  190.3 35.3 %fusion.73 = f32[1,1536,128]{1,2,0:T(8,128)S(1)} fusion(f32[128,1536]{1,0:T(8,128)S(1)} %fusion.8, f32[2,1536,6144]{2,1,0:T(8,128)} %param.6, f32[1,2,6144,128]{3,2,1,0:T(8,128)S(1)} %copy-done.2), kind=kOutput, calls=%fused_computation.79 | convolution fusion | flops 14495711232 | bytes 42467328 | tf_op jit(solution)/shard_map/dot_general | solution.py:18
  225.6 35.6 %fusion.67 = f32[1,1536,128]{1,2,0:T(8,128)S(1)} fusion(f32[128,1536]{1,0:T(8,128)S(1)} %fusion.10, f32[2,1536,6144]{2,1,0:T(8,128)} %param.6, f32[1,2,6144,128]{3,2,1,0:T(8,128)S(1)} %copy-done.2), kind=kOutput, calls=%fused_computation.77 | convolution fusion | flops 14495711232 | bytes 42467328 | tf_op jit(solution)/shard_map/dot_general | solution.py:18
  261.3 36.6 %fusion.4 = f32[128,1536]{1,0:T(8,128)S(1)} fusion(f32[2,1536,6144]{2,1,0:T(8,128)} %param.6, f32[1,2,6144,128]{3,2,1,0:T(8,128)} %all-gather.13.cloned.1.call-done), kind=kOutput, calls=%fused_computation.9 | convolution fusion | flops 14495514624 | bytes 41680896 | tf_op jit(solution)/shard_map/dot_general | solution.py:18
  297.9 35.2 %fusion.6 = f32[128,1536]{1,0:T(8,128)S(1)} fusion(f32[2,1536,6144]{2,1,0:T(8,128)} %param.6, f32[1,2,6144,128]{3,2,1,0:T(8,128)S(1)} %copy-done.3), kind=kOutput, calls=%fused_computation.11 | convolution fusion | flops 14495514624 | bytes 41680896 | tf_op jit(solution)/shard_map/dot_general | solution.py:18
  334.4 35.2 %fusion.85 = f32[1,1536,128]{1,2,0:T(8,128)S(1)} fusion(f32[128,1536]{1,0:T(8,128)S(1)} %fusion.4, f32[2,1536,6144]{2,1,0:T(8,128)} %param.6, f32[1,2,6144,128]{3,2,1,0:T(8,128)S(1)} %copy-done.3), kind=kOutput, calls=%fused_computation.83 | convolution fusion | flops 14495711232 | bytes 42467328 | tf_op jit(solution)/shard_map/dot_general | solution.py:18
  369.6 35.0 %fusion.79 = f32[1,1536,128]{1,2,0:T(8,128)S(1)} fusion(f32[128,1536]{1,0:T(8,128)S(1)} %fusion.6, f32[2,1536,6144]{2,1,0:T(8,128)} %param.6, f32[1,2,6144,128]{3,2,1,0:T(8,128)S(1)} %copy-done.3), kind=kOutput, calls=%fused_computation.81 | convolution fusion | flops 14495711232 | bytes 42467328 | tf_op jit(solution)/shard_map/dot_general | solution.py:18
  405.9 36.3 %fusion = f32[128,1536]{1,0:T(8,128)S(1)} fusion(f32[2,1536,6144]{2,1,0:T(8,128)} %param.6, f32[1,2,6144,128]{3,2,1,0:T(8,128)} %all-gather.15.cloned.1.call-done), kind=kOutput, calls=%fused_computation.5 | convolution fusion | flops 14495514624 | bytes 41680896 | tf_op jit(solution)/shard_map/dot_general | solution.py:18
  442.3 35.0 %fusion.2 = f32[128,1536]{1,0:T(8,128)S(1)} fusion(f32[2,1536,6144]{2,1,0:T(8,128)} %param.6, f32[1,2,6144,128]{3,2,1,0:T(8,128)S(1)} %copy-done.4), kind=kOutput, calls=%fused_computation.7 | convolution fusion | flops 14495514624 | bytes 41680896 | tf_op jit(solution)/shard_map/dot_general | solution.py:18
  477.3 35.5 %fusion.97 = f32[1,1536,128]{1,2,0:T(8,128)S(1)} fusion(f32[128,1536]{1,0:T(8,128)S(1)} %fusion, f32[2,1536,6144]{2,1,0:T(8,128)} %param.6, f32[1,2,6144,128]{3,2,1,0:T(8,128)S(1)} %copy-done.4), kind=kOutput, calls=%fused_computation.87 | convolution fusion | flops 14495711232 | bytes 42467328 | tf_op jit(solution)/shard_map/dot_general | solution.py:18
  512.8 35.0 %fusion.91 = f32[1,1536,128]{1,2,0:T(8,128)S(1)} fusion(f32[128,1536]{1,0:T(8,128)S(1)} %fusion.2, f32[2,1536,6144]{2,1,0:T(8,128)} %param.6, f32[1,2,6144,128]{3,2,1,0:T(8,128)S(1)} %copy-done.4), kind=kOutput, calls=%fused_computation.85 | convolution fusion | flops 14495711232 | bytes 42467328 | tf_op jit(solution)/shard_map/dot_general | solution.py:18
  549.1 36.3 %fusion.12 = f32[128,1536]{1,0:T(8,128)S(1)} fusion(f32[2,1536,6144]{2,1,0:T(8,128)} %param.6, f32[1,2,6144,128]{3,2,1,0:T(8,128)} %all-gather.9.cloned.1.call-done), kind=kOutput, calls=%fused_computation.17 | convolution fusion | flops 14495514624 | bytes 41680896 | tf_op jit(solution)/shard_map/dot_general | solution.py:18
  585.4 35.0 %fusion.14 = f32[128,1536]{1,0:T(8,128)S(1)} fusion(f32[2,1536,6144]{2,1,0:T(8,128)} %param.6, f32[1,2,6144,128]{3,2,1,0:T(8,128)S(1)} %copy-done.5), kind=kOutput, calls=%fused_computation.19 | convolution fusion | flops 14495514624 | bytes 41680896 | tf_op jit(solution)/shard_map/dot_general | solution.py:18
  620.5 35.5 %fusion.61 = f32[1,1536,128]{1,2,0:T(8,128)S(1)} fusion(f32[128,1536]{1,0:T(8,128)S(1)} %fusion.12, f32[2,1536,6144]{2,1,0:T(8,128)} %param.6, f32[1,2,6144,128]{3,2,1,0:T(8,128)S(1)} %copy-done.5), kind=kOutput, calls=%fused_computation.75 | convolution fusion | flops 14495711232 | bytes 42467328 | tf_op jit(solution)/shard_map/dot_general | solution.py:18
  655.9 35.0 %fusion.55 = f32[1,1536,128]{1,2,0:T(8,128)S(1)} fusion(f32[128,1536]{1,0:T(8,128)S(1)} %fusion.14, f32[2,1536,6144]{2,1,0:T(8,128)} %param.6, f32[1,2,6144,128]{3,2,1,0:T(8,128)S(1)} %copy-done.5), kind=kOutput, calls=%fused_computation.73 | convolution fusion | flops 14495711232 | bytes 42467328 | tf_op jit(solution)/shard_map/dot_general | solution.py:18
  694.0 2.2 dynamic-slice_multiply_fusion.1
  696.2 2.3 dynamic-slice_multiply_fusion
  698.5 2.5 dynamic-slice_multiply_fusion.3
  701.1 2.9 pad_maximum_fusion.1
  704.5 1.7 gather_fusion.2
  709.7 13.4 %all-reduce.7.cloned.1.call-done = (f32[2,1536,128]{1,2,0:T(8,128)}, f32[2,1536,128]{1,2,0:T(8,128)}, f32[2,1536,128]{1,2,0:T(8,128)}, f32[2,1536,128]{1,2,0:T(8,128)}) async-done(((f32[2,1536,128]{1,2,0:T(8,128)}, f32[2,1536,128]{1,2,0:T(8,128)}, f32[2,1536,128]{1,2,0:T(8,128)}, f32[2,1536,128]{1,2,0:T(8,128)}), (f32[2,1536,128]{1,2,0:T(8,128)}, f32[2,1536,128]{1,2,0:T(8,128)}, f32[2,1536,128]{1,2,0:T(8,128)}, ...) | async-done | bytes 6291472 | tf_op jit(solution)/shard_map/psum | solution.py:66
  732.7 3.3 fusion.220
  760.9 4.3 pad_maximum_fusion
  765.2 6.6 copy.33
  771.8 3.2 broadcast_in_dim.45
  775.0 13.3 %scatter_fusion = f32[4,2,1536,128]{3,2,1,0:T(8,128)} fusion(f32[4,2,1536,128]{3,2,1,0:T(8,128)} %broadcast_in_dim.45, s32[4]{0:T(128)S(1)} %copy-done.32, f32[4,2,1536,128]{3,2,1,0:T(8,128)} %copy.33), kind=kCustom, calls=%fused_computation.3 | custom fusion | bytes 18874384 | tf_op jit(solution)/shard_map/scatter | solution.py:118
  788.3 66.6 %all-reduce.5.cloned.1.call-done = (f32[4,2,128,128]{3,2,1,0:T(8,128)}, f32[2,2,128,128]{3,2,1,0:T(8,128)}) async-done(((f32[4,2,128,128]{3,2,1,0:T(8,128)}, f32[2,2,128,128]{3,2,1,0:T(8,128)}), (f32[4,2,128,128]{3,2,1,0:T(8,128)}, f32[2,2,128,128]{3,2,1,0:T(8,128)})) %all-reduce.5.cloned.1.call-update) | async-done | bytes 786448 | tf_op jit(solution)/shard_map/psum | solution.py:104
  863.6 2.7 scatter_fusion.1
  (183 shorter events, 60.8 us)
Async XLA Ops:
  7.2 3.5 copy-start
  7.2 112.0 %all-gather.11.cloned.1.call-start = ((), (), s32[]{:S(2)}) async-start(), calls=%async_computation.1 | async-start | bytes 7077888 | tf_op jit(solution)/shard_map/all_gather | solution.py:64
  8.0 5.4 copy-start.33
  9.3 3.8 copy-start.30
  17.6 243.7 %all-gather.13.cloned.1.call-start = ((), (), s32[]{:S(2)}) async-start(), calls=%async_computation.2 | async-start | bytes 7077888 | tf_op jit(solution)/shard_map/all_gather | solution.py:64
  18.3 387.6 %all-gather.15.cloned.1.call-start = ((), (), s32[]{:S(2)}) async-start(), calls=%async_computation.3 | async-start | bytes 7077888 | tf_op jit(solution)/shard_map/all_gather | solution.py:64
  19.1 530.0 %all-gather.9.cloned.1.call-start = ((), (), s32[]{:S(2)}) async-start(), calls=%async_computation | async-start | bytes 7077888 | tf_op jit(solution)/shard_map/all_gather | solution.py:64
  19.7 703.5 %all-reduce.7.cloned.1.call-start = ((), (), s32[]{:S(2)}) async-start(), calls=%async_computation.5 | async-start | bytes 12582912 | tf_op jit(solution)/shard_map/psum | solution.py:66
  119.2 36.1 %copy-start.2 = (f32[1,2,6144,128]{3,2,1,0:T(8,128)S(1)}, f32[1,2,6144,128]{3,2,1,0:T(8,128)}, u32[]{:S(2)}) copy-start(f32[1,2,6144,128]{3,2,1,0:T(8,128)} %all-gather.11.cloned.1.call-done) | copy-start | bytes 18874372
  261.3 36.6 %copy-start.3 = (f32[1,2,6144,128]{3,2,1,0:T(8,128)S(1)}, f32[1,2,6144,128]{3,2,1,0:T(8,128)}, u32[]{:S(2)}) copy-start(f32[1,2,6144,128]{3,2,1,0:T(8,128)} %all-gather.13.cloned.1.call-done) | copy-start | bytes 18874372
  405.9 36.3 %copy-start.4 = (f32[1,2,6144,128]{3,2,1,0:T(8,128)S(1)}, f32[1,2,6144,128]{3,2,1,0:T(8,128)}, u32[]{:S(2)}) copy-start(f32[1,2,6144,128]{3,2,1,0:T(8,128)} %all-gather.15.cloned.1.call-done) | copy-start | bytes 18874372
  549.1 36.3 %copy-start.5 = (f32[1,2,6144,128]{3,2,1,0:T(8,128)S(1)}, f32[1,2,6144,128]{3,2,1,0:T(8,128)}, u32[]{:S(2)}) copy-start(f32[1,2,6144,128]{3,2,1,0:T(8,128)} %all-gather.9.cloned.1.call-done) | copy-start | bytes 18874372
  692.3 162.6 %all-reduce.5.cloned.1.call-start = ((), (), s32[]{:S(2)}) async-start(), calls=%async_computation.4 | async-start | bytes 1572864 | tf_op jit(solution)/shard_map/psum | solution.py:104
  694.0 7.1 copy-start.10
  696.2 4.9 copy-start.12
  698.5 5.5 copy-start.14
  701.1 5.2 copy-start.35
  701.1 5.2 copy-start.37
  701.1 6.4 copy-start.18
  704.5 27.2 %collective-permute-start = (f32[4,2,1536,128]{3,2,1,0:T(8,128)}, f32[4,2,1536,128]{3,2,1,0:T(8,128)}, u32[]{:S(2)}, u32[]{:S(2)}) collective-permute-start(f32[4,2,1536,128]{3,2,1,0:T(8,128)} %pad_maximum_fusion.1), channel_id=1, source_target_pairs={{0,1},{1,0},{2,3},{3,2},{4,5},{5,4},{6,7},{7,6},{8,9},{9,8},{10,11... | collective-permute-start | bytes 18874376 | tf_op jit(solution)/shard_map/ppermute | solution.py:14
  725.3 3.4 copy-start.20
  728.8 3.5 copy-start.15
  728.8 3.9 copy-start.17
  746.2 9.5 %copy-start.8 = (f32[2,1536,128]{1,2,0:T(8,128)}, f32[2,1536,128]{1,2,0:T(8,128)S(1)}, u32[]{:S(2)}) copy-start(f32[2,1536,128]{1,2,0:T(8,128)S(1)} %get-tuple-element.36) | copy-start | bytes 4718596
  746.2 11.1 %copy-start.6 = (f32[2,1536,128]{1,2,0:T(8,128)}, f32[2,1536,128]{1,2,0:T(8,128)S(1)}, u32[]{:S(2)}) copy-start(f32[2,1536,128]{1,2,0:T(8,128)S(1)} %get-tuple-element.35) | copy-start | bytes 4718596
  757.3 3.5 copy-start.9
  775.0 79.9 %copy-start.21 = (f32[4,2,128,128]{3,2,1,0:T(8,128)S(1)}, f32[4,2,128,128]{3,2,1,0:T(8,128)}, u32[]{:S(2)}) copy-start(f32[4,2,128,128]{3,2,1,0:T(8,128)} %broadcast_select_fusion) | copy-start | bytes 1572868
  788.3 70.4 %copy-start.26 = (f32[2,128,128]{1,2,0:T(8,128)S(1)}, f32[2,128,128]{1,2,0:T(8,128)}, u32[]{:S(2)}) copy-start(f32[2,128,128]{1,2,0:T(8,128)} %get-tuple-element.31) | copy-start | bytes 393220
  854.9 5.0 copy-start.27
  854.9 6.2 copy-start.22
  854.9 6.2 copy-start.25
  859.9 6.4 copy-start.1
  (13 other events, 29.3 us)
Sparse Core Ops, SparseCore 0:
  17.7 101.4 all-gather.10
  121.4 96.8 all-gather.12
  220.5 96.9 all-gather.14
  320.1 96.8 all-gather.8
  692.4 30.6 all-reduce.6
  761.0 93.8 all-reduce.4
where the time goes:
time: 883 us; the launch traced here: 874 us
  matrix products  597 us (68%)
  waiting for transfers between devices  181 us (20%)
  other arithmetic  41.3 us (5%)
  local copies, waits for them, and re-layouts  38.3 us (4%)
  between operations  15.6 us (2%)
    dot_general x66, matrix products, matmul(): jnp.dot(left_side, right_side, preferred_element_type=jnp.float32, precis...  597 us
    all_gather x4, waiting for transfers between devices, per_device(): gathered = lax.all_gather(panels[tree_slot], 'row', axis=1, tiled=True)  99.5 us
    psum x1, waiting for transfers between devices, per_device(): lax.psum(jnp.stack(cross_local + child_local), ('row', 'col'))  66.6 us
  transfers between devices with their start and end apart: 7, of which 3 were waited for; matrix products, arithmetic and copies ran while one was open for 55% of the time, Pallas kernels for 0%

commit v1 on v0

--- a/solution.py
+++ b/solution.py
@@ -101,7 +101,9 @@
     ]
     parent_sums = lax.psum(jnp.stack(parent_local), ("row", "col"))
     parent_diag = [diag_blocks[tree_slot] - parent_sums[tree_slot] for tree_slot in range(2)]
-    child_totals = lax.psum(jnp.stack(cross_local + child_local), ("row", "col"))
+    child_totals = jnp.sum(
+        lax.all_gather(jnp.stack(cross_local + child_local), ("row", "col")), axis=0
+    )
     crosses = [
         -(child_totals[tree_slot] + multiply(parent_diag[tree_slot], coupling[tree_slot]))
         for tree_slot in range(2)

time: 883 us -> 954 us (1.080)
  waiting for transfers between devices: 181 us -> 240 us
    all_gather x0 -> x1, waiting for transfers between devices: none -> 74.2 us  [per_device(): lax.all_gather(jnp.stack(cross_local + child_local), ('row', 'col'))]
    psum x1, waiting for transfers between devices: 66.6 us -> 46.2 us  [per_device(): parent_sums = lax.psum(jnp.stack(parent_local), ('row', 'col'))]
  transfers between devices with their start and end apart: 7 -> 8, of which waited for: 3 -> 4; matrix products, arithmetic and copies ran while one was open for 55% -> 52% of each run, Pallas kernels for 0% -> 0%
where the time goes in v1:
time: 954 us; the launch traced here: 944 us
  matrix products  606 us (64%)
  waiting for transfers between devices  240 us (25%)
  other arithmetic  43.2 us (5%)
  local copies, waits for them, and re-layouts  39.3 us (4%)
  between operations  15.8 us (2%)
    dot_general x66, matrix products, matmul(): jnp.dot(left_side, right_side, preferred_element_type=jnp.float32, precis...  606 us
    all_gather x4, waiting for transfers between devices, per_device(): gathered = lax.all_gather(panels[tree_slot], 'row', axis=1, tiled=True)  99.5 us
    all_gather x1, waiting for transfers between devices, per_device(): lax.all_gather(jnp.stack(cross_local + child_local), ('row', 'col'))  74.2 us
    psum x1, waiting for transfers between devices, per_device(): parent_sums = lax.psum(jnp.stack(parent_local), ('row', 'col'))  46.2 us
  transfers between devices with their start and end apart: 8, of which 4 were waited for; matrix products, arithmetic and copies ran while one was open for 52% of the time, Pallas kernels for 0%

profile of v1, /device:TPU:0, one launch (start us, length us, event | category | flops | bytes accessed | tf_op | source)
XLA Modules:
  0.0 944.4 jit_solution(13649763030751587616)
XLA Ops:
  10.7 2.4 gather_fusion.1
  13.5 2.4 select_multiply_fusion
  19.8 99.5 %all-gather.13.cloned.1.call-done = f32[1,2,6144,128]{3,2,1,0:T(8,128)} async-done(((f32[1,2,768,128]{3,2,1,0:T(8,128)}), f32[1,2,6144,128]{3,2,1,0:T(8,128)}) %all-gather.13.cloned.1.call-update) | async-done | bytes 6291472 | tf_op jit(solution)/shard_map/all_gather | solution.py:64
  119.3 36.1 %fusion.8 = f32[128,1536]{1,0:T(8,128)S(1)} fusion(f32[2,1536,6144]{2,1,0:T(8,128)} %param.6, f32[1,2,6144,128]{3,2,1,0:T(8,128)} %all-gather.13.cloned.1.call-done), kind=kOutput, calls=%fused_computation.13 | convolution fusion | flops 14495514624 | bytes 41680896 | tf_op jit(solution)/shard_map/dot_general | solution.py:18
  155.4 35.0 %fusion.10 = f32[128,1536]{1,0:T(8,128)S(1)} fusion(f32[2,1536,6144]{2,1,0:T(8,128)} %param.6, f32[1,2,6144,128]{3,2,1,0:T(8,128)S(1)} %copy-done.2), kind=kOutput, calls=%fused_computation.15 | convolution fusion | flops 14495514624 | bytes 41680896 | tf_op jit(solution)/shard_map/dot_general | solution.py:18
  190.4 35.3 %fusion.73 = f32[1,1536,128]{1,2,0:T(8,128)S(1)} fusion(f32[128,1536]{1,0:T(8,128)S(1)} %fusion.8, f32[2,1536,6144]{2,1,0:T(8,128)} %param.6, f32[1,2,6144,128]{3,2,1,0:T(8,128)S(1)} %copy-done.2), kind=kOutput, calls=%fused_computation.79 | convolution fusion | flops 14495711232 | bytes 42467328 | tf_op jit(solution)/shard_map/dot_general | solution.py:18
  225.7 35.6 %fusion.67 = f32[1,1536,128]{1,2,0:T(8,128)S(1)} fusion(f32[128,1536]{1,0:T(8,128)S(1)} %fusion.10, f32[2,1536,6144]{2,1,0:T(8,128)} %param.6, f32[1,2,6144,128]{3,2,1,0:T(8,128)S(1)} %copy-done.2), kind=kOutput, calls=%fused_computation.77 | convolution fusion | flops 14495711232 | bytes 42467328 | tf_op jit(solution)/shard_map/dot_general | solution.py:18
  261.4 36.5 %fusion.4 = f32[128,1536]{1,0:T(8,128)S(1)} fusion(f32[2,1536,6144]{2,1,0:T(8,128)} %param.6, f32[1,2,6144,128]{3,2,1,0:T(8,128)} %all-gather.15.cloned.1.call-done), kind=kOutput, calls=%fused_computation.9 | convolution fusion | flops 14495514624 | bytes 41680896 | tf_op jit(solution)/shard_map/dot_general | solution.py:18
  297.9 35.2 %fusion.6 = f32[128,1536]{1,0:T(8,128)S(1)} fusion(f32[2,1536,6144]{2,1,0:T(8,128)} %param.6, f32[1,2,6144,128]{3,2,1,0:T(8,128)S(1)} %copy-done.3), kind=kOutput, calls=%fused_computation.11 | convolution fusion | flops 14495514624 | bytes 41680896 | tf_op jit(solution)/shard_map/dot_general | solution.py:18
  334.4 35.2 %fusion.85 = f32[1,1536,128]{1,2,0:T(8,128)S(1)} fusion(f32[128,1536]{1,0:T(8,128)S(1)} %fusion.4, f32[2,1536,6144]{2,1,0:T(8,128)} %param.6, f32[1,2,6144,128]{3,2,1,0:T(8,128)S(1)} %copy-done.3), kind=kOutput, calls=%fused_computation.83 | convolution fusion | flops 14495711232 | bytes 42467328 | tf_op jit(solution)/shard_map/dot_general | solution.py:18
  369.6 35.1 %fusion.79 = f32[1,1536,128]{1,2,0:T(8,128)S(1)} fusion(f32[128,1536]{1,0:T(8,128)S(1)} %fusion.6, f32[2,1536,6144]{2,1,0:T(8,128)} %param.6, f32[1,2,6144,128]{3,2,1,0:T(8,128)S(1)} %copy-done.3), kind=kOutput, calls=%fused_computation.81 | convolution fusion | flops 14495711232 | bytes 42467328 | tf_op jit(solution)/shard_map/dot_general | solution.py:18
  406.0 36.3 %fusion = f32[128,1536]{1,0:T(8,128)S(1)} fusion(f32[2,1536,6144]{2,1,0:T(8,128)} %param.6, f32[1,2,6144,128]{3,2,1,0:T(8,128)} %all-gather.17.cloned.1.call-done), kind=kOutput, calls=%fused_computation.5 | convolution fusion | flops 14495514624 | bytes 41680896 | tf_op jit(solution)/shard_map/dot_general | solution.py:18
  442.3 35.0 %fusion.2 = f32[128,1536]{1,0:T(8,128)S(1)} fusion(f32[2,1536,6144]{2,1,0:T(8,128)} %param.6, f32[1,2,6144,128]{3,2,1,0:T(8,128)S(1)} %copy-done.4), kind=kOutput, calls=%fused_computation.7 | convolution fusion | flops 14495514624 | bytes 41680896 | tf_op jit(solution)/shard_map/dot_general | solution.py:18
  477.3 35.5 %fusion.97 = f32[1,1536,128]{1,2,0:T(8,128)S(1)} fusion(f32[128,1536]{1,0:T(8,128)S(1)} %fusion, f32[2,1536,6144]{2,1,0:T(8,128)} %param.6, f32[1,2,6144,128]{3,2,1,0:T(8,128)S(1)} %copy-done.4), kind=kOutput, calls=%fused_computation.87 | convolution fusion | flops 14495711232 | bytes 42467328 | tf_op jit(solution)/shard_map/dot_general | solution.py:18
  512.8 35.0 %fusion.91 = f32[1,1536,128]{1,2,0:T(8,128)S(1)} fusion(f32[128,1536]{1,0:T(8,128)S(1)} %fusion.2, f32[2,1536,6144]{2,1,0:T(8,128)} %param.6, f32[1,2,6144,128]{3,2,1,0:T(8,128)S(1)} %copy-done.4), kind=kOutput, calls=%fused_computation.85 | convolution fusion | flops 14495711232 | bytes 42467328 | tf_op jit(solution)/shard_map/dot_general | solution.py:18
  549.1 36.3 %fusion.12 = f32[128,1536]{1,0:T(8,128)S(1)} fusion(f32[2,1536,6144]{2,1,0:T(8,128)} %param.6, f32[1,2,6144,128]{3,2,1,0:T(8,128)} %all-gather.11.cloned.1.call-done), kind=kOutput, calls=%fused_computation.17 | convolution fusion | flops 14495514624 | bytes 41680896 | tf_op jit(solution)/shard_map/dot_general | solution.py:18
  585.4 35.0 %fusion.14 = f32[128,1536]{1,0:T(8,128)S(1)} fusion(f32[2,1536,6144]{2,1,0:T(8,128)} %param.6, f32[1,2,6144,128]{3,2,1,0:T(8,128)S(1)} %copy-done.5), kind=kOutput, calls=%fused_computation.19 | convolution fusion | flops 14495514624 | bytes 41680896 | tf_op jit(solution)/shard_map/dot_general | solution.py:18
  620.5 35.5 %fusion.61 = f32[1,1536,128]{1,2,0:T(8,128)S(1)} fusion(f32[128,1536]{1,0:T(8,128)S(1)} %fusion.12, f32[2,1536,6144]{2,1,0:T(8,128)} %param.6, f32[1,2,6144,128]{3,2,1,0:T(8,128)S(1)} %copy-done.5), kind=kOutput, calls=%fused_computation.75 | convolution fusion | flops 14495711232 | bytes 42467328 | tf_op jit(solution)/shard_map/dot_general | solution.py:18
  655.9 35.0 %fusion.55 = f32[1,1536,128]{1,2,0:T(8,128)S(1)} fusion(f32[128,1536]{1,0:T(8,128)S(1)} %fusion.14, f32[2,1536,6144]{2,1,0:T(8,128)} %param.6, f32[1,2,6144,128]{3,2,1,0:T(8,128)S(1)} %copy-done.5), kind=kOutput, calls=%fused_computation.73 | convolution fusion | flops 14495711232 | bytes 42467328 | tf_op jit(solution)/shard_map/dot_general | solution.py:18
  698.5 2.5 dynamic-slice_multiply_fusion.3
  701.0 3.0 pad_maximum_fusion.1
  705.2 17.9 %all-reduce.6.cloned.1.call-done = (f32[2,1536,128]{1,2,0:T(8,128)}, f32[2,1536,128]{1,2,0:T(8,128)}, f32[2,1536,128]{1,2,0:T(8,128)}, f32[2,1536,128]{1,2,0:T(8,128)}) async-done(((f32[2,1536,128]{1,2,0:T(8,128)}, f32[2,1536,128]{1,2,0:T(8,128)}, f32[2,1536,128]{1,2,0:T(8,128)}, f32[2,1536,128]{1,2,0:T(8,128)}), (f32[2,1536,128]{1,2,0:T(8,128)}, f32[2,1536,128]{1,2,0:T(8,128)}, f32[2,1536,128]{1,2,0:T(8,128)}, ...) | async-done | bytes 6291472 | tf_op jit(solution)/shard_map/psum | solution.py:66
  729.4 3.4 fusion.220
  767.2 2.5 gather_fusion.2
  774.2 3.2 pad_maximum_fusion
  777.4 6.6 copy.50
  784.0 3.2 broadcast_in_dim.45
  787.2 13.1 %scatter_fusion = f32[4,2,1536,128]{3,2,1,0:T(8,128)} fusion(f32[4,2,1536,128]{3,2,1,0:T(8,128)} %broadcast_in_dim.45, s32[4]{0:T(128)S(1)} %copy-done.46, f32[4,2,1536,128]{3,2,1,0:T(8,128)} %copy.50), kind=kCustom, calls=%fused_computation.3 | custom fusion | bytes 18874384 | tf_op jit(solution)/shard_map/scatter | solution.py:120
  800.3 46.2 %all-reduce.4.cloned.1.call-done = f32[2,2,128,128]{3,2,1,0:T(8,128)} async-done(((f32[2,2,128,128]{3,2,1,0:T(8,128)}), f32[2,2,128,128]{3,2,1,0:T(8,128)}) %all-reduce.4.cloned.1.call-update) | async-done | bytes 262160 | tf_op jit(solution)/shard_map/psum | solution.py:102
  849.2 74.2 %all-gather.19.cloned.1.call-done = f32[64,2,128,128]{3,2,1,0:T(8,128)} async-done(((f32[4,2,128,128]{3,2,1,0:T(8,128)}), f32[64,2,128,128]{3,2,1,0:T(8,128)}) %all-gather.19.cloned.1.call-update) | async-done | bytes 8388624 | tf_op jit(solution)/shard_map/all_gather | solution.py:105
  923.4 4.0 reduce_sum.9
  934.5 2.7 scatter_fusion.1
  (217 shorter events, 74.2 us)
Async XLA Ops:
  7.2 112.1 %all-gather.13.cloned.1.call-start = ((), (), s32[]{:S(2)}) async-start(), calls=%async_computation.2 | async-start | bytes 7077888 | tf_op jit(solution)/shard_map/all_gather | solution.py:64
  17.7 243.7 %all-gather.15.cloned.1.call-start = ((), (), s32[]{:S(2)}) async-start(), calls=%async_computation.3 | async-start | bytes 7077888 | tf_op jit(solution)/shard_map/all_gather | solution.py:64
  18.4 387.5 %all-gather.17.cloned.1.call-start = ((), (), s32[]{:S(2)}) async-start(), calls=%async_computation.4 | async-start | bytes 7077888 | tf_op jit(solution)/shard_map/all_gather | solution.py:64
  19.2 529.9 %all-gather.11.cloned.1.call-start = ((), (), s32[]{:S(2)}) async-start(), calls=%async_computation.1 | async-start | bytes 7077888 | tf_op jit(solution)/shard_map/all_gather | solution.py:64
  19.7 703.4 %all-reduce.6.cloned.1.call-start = ((), (), s32[]{:S(2)}) async-start(), calls=%async_computation.6 | async-start | bytes 12582912 | tf_op jit(solution)/shard_map/psum | solution.py:66
  119.3 36.1 %copy-start.2 = (f32[1,2,6144,128]{3,2,1,0:T(8,128)S(1)}, f32[1,2,6144,128]{3,2,1,0:T(8,128)}, u32[]{:S(2)}) copy-start(f32[1,2,6144,128]{3,2,1,0:T(8,128)} %all-gather.13.cloned.1.call-done) | copy-start | bytes 18874372
  261.4 36.6 %copy-start.3 = (f32[1,2,6144,128]{3,2,1,0:T(8,128)S(1)}, f32[1,2,6144,128]{3,2,1,0:T(8,128)}, u32[]{:S(2)}) copy-start(f32[1,2,6144,128]{3,2,1,0:T(8,128)} %all-gather.15.cloned.1.call-done) | copy-start | bytes 18874372
  406.0 36.3 %copy-start.4 = (f32[1,2,6144,128]{3,2,1,0:T(8,128)S(1)}, f32[1,2,6144,128]{3,2,1,0:T(8,128)}, u32[]{:S(2)}) copy-start(f32[1,2,6144,128]{3,2,1,0:T(8,128)} %all-gather.17.cloned.1.call-done) | copy-start | bytes 18874372
  549.1 36.3 %copy-start.5 = (f32[1,2,6144,128]{3,2,1,0:T(8,128)S(1)}, f32[1,2,6144,128]{3,2,1,0:T(8,128)}, u32[]{:S(2)}) copy-start(f32[1,2,6144,128]{3,2,1,0:T(8,128)} %all-gather.11.cloned.1.call-done) | copy-start | bytes 18874372
  692.3 154.2 %all-reduce.4.cloned.1.call-start = ((), (), s32[]{:S(2)}) async-start(), calls=%async_computation | async-start | bytes 524288 | tf_op jit(solution)/shard_map/psum | solution.py:102
  694.0 7.0 copy-start.10
  704.5 24.9 %collective-permute-start = (f32[4,2,1536,128]{3,2,1,0:T(8,128)}, f32[4,2,1536,128]{3,2,1,0:T(8,128)}, u32[]{:S(2)}, u32[]{:S(2)}) collective-permute-start(f32[4,2,1536,128]{3,2,1,0:T(8,128)} %pad_maximum_fusion.1), channel_id=1, source_target_pairs={{0,1},{1,0},{2,3},{3,2},{4,5},{5,4},{6,7},{7,6},{8,9},{9,8},{10,11... | collective-permute-start | bytes 18874376 | tf_op jit(solution)/shard_map/ppermute | solution.py:14
  725.9 11.1 %copy-start.23 = (f32[2,128,768]{2,1,0:T(8,128)}, f32[2,128,768]{2,1,0:T(8,128)S(1)}, u32[]{:S(2)}) copy-start(f32[2,128,768]{2,1,0:T(8,128)S(1)} %get-tuple-element.39) | copy-start | bytes 2359300
  725.9 24.3 %copy-start.21 = (f32[2,128,768]{2,1,0:T(8,128)}, f32[2,128,768]{2,1,0:T(8,128)S(1)}, u32[]{:S(2)}) copy-start(f32[2,128,768]{2,1,0:T(8,128)S(1)} %get-tuple-element.40) | copy-start | bytes 2359300
  733.2 8.7 copy-start.20
  733.2 17.0 %copy-start.18 = (f32[1,2,1536,128]{3,2,1,0:T(8,128)}, f32[1,2,1536,128]{3,2,1,0:T(8,128)S(1)}, u32[]{:S(2)}) copy-start(f32[1,2,1536,128]{3,2,1,0:T(8,128)S(1)} %get-tuple-element.13) | copy-start | bytes 4718596
  743.6 9.4 copy-start.6
  743.6 9.4 copy-start.8
  753.8 8.7 copy-start.7
  755.4 168.0 %all-gather.19.cloned.1.call-start = ((), (), s32[]{:S(2)}) async-start(), calls=%async_computation.5 | async-start | bytes 8912896 | tf_op jit(solution)/shard_map/all_gather | solution.py:105
  755.5 8.9 copy-start.25
  755.5 8.9 copy-start.42
  755.5 9.7 %copy-start.19 = (f32[1,2,1536,128]{3,2,1,0:T(8,128)S(1)}, f32[1,2,1536,128]{3,2,1,0:T(8,128)}, u32[]{:S(2)}) copy-start(f32[1,2,1536,128]{3,2,1,0:T(8,128)} %copy-done.18) | copy-start | bytes 4718596
  755.5 9.7 %copy-start.22 = (f32[2,128,768]{2,1,0:T(8,128)S(1)}, f32[2,128,768]{2,1,0:T(8,128)}, u32[]{:S(2)}) copy-start(f32[2,128,768]{2,1,0:T(8,128)} %copy-done.21) | copy-start | bytes 2359300
  755.5 10.2 %copy-start.43 = (f32[128,128]{1,0:T(8,128)S(1)}, f32[128,128]{1,0:T(8,128)}, u32[]{:S(2)}) copy-start(f32[128,128]{1,0:T(8,128)} %fusion.130) | copy-start | bytes 196612
  787.2 59.3 %copy-start.31 = (f32[4,2,128,128]{3,2,1,0:T(8,128)S(1)}, f32[4,2,128,128]{3,2,1,0:T(8,128)}, u32[]{:S(2)}) copy-start(f32[4,2,128,128]{3,2,1,0:T(8,128)} %broadcast_select_fusion) | copy-start | bytes 1572868
  847.5 80.0 %copy-start.32 = (f32[1,2,128,128]{3,2,1,0:T(8,128)}, f32[1,2,128,128]{3,2,1,0:T(8,128)S(1)}, u32[]{:S(2)}) copy-start(f32[1,2,128,128]{3,2,1,0:T(8,128)S(1)} %get-tuple-element.22) | copy-start | bytes 393220
  848.5 78.9 %copy-start.38 = (f32[128,128]{1,0:T(8,128)}, f32[128,128]{1,0:T(8,128)S(1)}, u32[]{:S(2)}) copy-start(f32[128,128]{1,0:T(8,128)S(1)} %convolution_add_fusion.5) | copy-start | bytes 196612
  848.8 78.7 %copy-start.39 = (f32[128,128]{1,0:T(8,128)}, f32[128,128]{1,0:T(8,128)S(1)}, u32[]{:S(2)}) copy-start(f32[128,128]{1,0:T(8,128)S(1)} %convolution_subtract_fusion.5) | copy-start | bytes 196612
  849.0 78.5 %copy-start.40 = (f32[128,128]{1,0:T(8,128)}, f32[128,128]{1,0:T(8,128)S(1)}, u32[]{:S(2)}) copy-start(f32[128,128]{1,0:T(8,128)S(1)} %convolution_add_fusion.3) | copy-start | bytes 196612
  849.2 78.3 %copy-start.41 = (f32[128,128]{1,0:T(8,128)}, f32[128,128]{1,0:T(8,128)S(1)}, u32[]{:S(2)}) copy-start(f32[128,128]{1,0:T(8,128)S(1)} %convolution_subtract_fusion.3) | copy-start | bytes 196612
  929.5 7.7 copy-start.1
  (29 other events, 101.4 us)
Sparse Core Ops, SparseCore 0:
  17.8 101.4 all-gather.12
  121.4 96.8 all-gather.14
  220.6 96.9 all-gather.16
  320.1 96.8 all-gather.10
  692.4 30.6 all-reduce.5
  755.5 90.8 all-reduce.3
  848.6 74.7 all-gather.18
